TPU v7x, 256 devices: a whole 4x4x8 slice. The times are simulated.
256 devices in a mesh: tok: 32 (over y, x, core), rep: 8 (over z).
Axes of the slice: x: 4, y: 4, z: 8, core: 2. Of those that a mesh axis runs over, the one named last changes fastest.
Arguments:
- hidden_states: bfloat16 [8, 4096, 2048], P('rep', 'tok'), may hold values from -6 to 6
- routes: int32 [8, 4096, 8], P('rep', 'tok'), may hold values from 0 to 31, all different within a row; in each aligned block of 128 rows (0 to 127, 128 to 255, ..., all dimensions but the last counted through in order) at most 36 rows name the same one
- gate_prob: float32 [8, 4096, 8], P('rep', 'tok'), may hold values from 0.03 to 0.3
- gate_up: float32 [32, 2048, 2048], P('tok', 'rep'), may hold values from -0.125 to 0.125
- down: float32 [32, 1024, 2048], P('tok', 'rep'), may hold values from -0.1875 to 0.1875
Outputs:
- mixed: bfloat16 [8, 4096, 2048], P('rep', 'tok')
Inputs may be any that keep to these rules, and one draw needn't show every extreme that they name: `routes`: each row names 8 different experts. No expert is named by more than 36 rows of one device's 128 tokens, and some expert reaches 36 on some devices.
All inputs are finite; a program needn't handle non-finite values.
Results may differ from a plain program's by a relative error of at most 0.012.
Values may be sent and summed in bfloat16 or wider, within the bound.
No kernel may reach another device: no remote copies, remote signals or barrier semaphores. Data moves between devices by JAX's collectives and lax.ppermute only.
A program may use at most 128 MiB of HBM per device.

v0:
```python
import jax
import jax.numpy as jnp
from jax import lax
from jax.sharding import PartitionSpec as P

CAP = 36


def per_device(hidden_states, routes, gate_prob, gate_up, down):
    groups = lax.axis_size("tok")
    local_experts = gate_up.shape[0]
    model_width = hidden_states.shape[2]
    token_count = hidden_states.shape[1]
    top_count = routes.shape[2]
    all_experts = groups * local_experts
    capacity = CAP
    served_gate = gate_up.astype(jnp.bfloat16)
    served_down = down.astype(jnp.bfloat16)
    unit_count = served_gate.shape[2] // 2
    full_gate, full_down = (
        lax.all_gather(served_gate, "rep", axis=1, tiled=True),
        lax.all_gather(served_down, "rep", axis=1, tiled=True),
    )
    flat_picks = routes[0].reshape(-1)
    pick_count = flat_picks.shape[0]
    one_hot = (flat_picks[:, None] == jnp.arange(all_experts, dtype=jnp.int32)[None, :]).astype(
        jnp.int32
    )
    earlier = jnp.cumsum(one_hot, axis=0) - one_hot
    slot_index = jnp.sum(earlier * one_hot, axis=1)
    owners = jnp.arange(pick_count, dtype=jnp.int32) // top_count
    slot_table = (
        jnp.full((all_experts, capacity), token_count, jnp.int32)
        .at[flat_picks, slot_index]
        .set(owners)
    )
    padded_rows = jnp.concatenate(
        [hidden_states[0], jnp.zeros((1, model_width), jnp.bfloat16)], axis=0
    )
    send_rows = padded_rows[slot_table].reshape(groups, local_experts, capacity, model_width)
    arrived = lax.all_to_all(send_rows, "tok", split_axis=0, concat_axis=0, tiled=True)
    gate_both = jnp.einsum("secd,edf->secf", arrived, full_gate, preferred_element_type=jnp.float32)
    hidden_units = (jax.nn.silu(gate_both[..., :unit_count]) * gate_both[..., unit_count:]).astype(
        jnp.bfloat16
    )
    projected = jnp.einsum(
        "secf,efd->secd", hidden_units, full_down, preferred_element_type=jnp.float32
    )
    expert_out = projected.astype(jnp.bfloat16)
    returned = lax.all_to_all(expert_out, "tok", split_axis=0, concat_axis=0, tiled=True)
    returned = returned.reshape(all_experts, capacity, model_width)
    picked_rows = returned[flat_picks, slot_index].reshape(token_count, top_count, model_width)
    mixed_rows = jnp.einsum(
        "tk,tkd->td", gate_prob[0], picked_rows, preferred_element_type=jnp.float32
    )
    return mixed_rows.astype(jnp.bfloat16)[None]


def solution(mesh):
    return jax.shard_map(
        per_device,
        mesh=mesh,
        in_specs=(
            P("rep", "tok", None),
            P("rep", "tok", None),
            P("rep", "tok", None),
            P("tok", "rep", None),
            P("tok", "rep", None),
        ),
        out_specs=P("rep", "tok", None),
        check_vma=False,
    )
```

profile of v0, /device:TPU:7, one launch (start us, length us, event | category | flops | bytes accessed | tf_op | source)
XLA Modules:
  0.0 288.8 jit_solution(6611978452512759054)
XLA Ops:
  6.5 0.0 copy-start.4
  6.5 0.0 copy-start.3
  6.5 0.0 copy-start.1
  6.5 0.0 all-gather.3.cloned.1.call-start
  6.5 2.8 convert_element_type.33
  9.3 0.0 all-gather.3.cloned.1.call-update
  9.4 0.8 copy.13
  10.1 0.1 eq.29
  10.2 0.1 eq.25
  10.3 0.1 reshape_squeeze.3
  10.4 9.0 %reduce-window.6 = s32[32,8,128]{2,1,0:T(8,128)S(1)} reduce-window(s32[32,8,128]{2,1,0:T(8,128)S(1)} %fusion.21, s32[]{:T(128)} %constant.29.clone.1), window={size=1x1x128 pad=0_0x0_0x127_0}, to_apply=%region_0.0 | reduce-window | flops 4161536 | bytes 262148 | tf_op jit(solution)/shard_map/reduce-window
  19.5 0.1 slice.20
  19.6 0.1 copy.16
  19.7 0.1 copy.17
  19.8 0.1 broadcast_add_fusion
  20.0 0.0 copy-done.4
  20.0 0.1 multiply_reduce_fusion
  20.1 0.0 copy-done.3
  20.1 0.1 and_reduce_fusion
  20.2 4.3 %scatter_custom_fusion = s32[1152]{0:T(1024)S(1)} fusion(s32[1024]{0:T(1024)S(1)} %get-tuple-element.9, s32[1024]{0:T(1024)S(1)} %get-tuple-element.8, s32[]{:T(128)} %constant.28.clone.1), kind=kCustom, calls=%fused_computation.40 | custom fusion | bytes 4612
  24.5 0.1 reshape.93
  24.6 0.1 reshape.96
  24.7 0.0 copy-done.1
  24.8 6.0 %gather_fusion = bf16[1152,2048]{1,0:T(8,128)(2,1)} fusion(bf16[129,2048]{1,0:T(8,128)(2,1)S(1)} %concatenate.7, s32[2048]{0:T(1024)S(1)} %pad_clamp_fusion), kind=kCustom, calls=%fused_computation | custom fusion | bytes 9441792 | tf_op jit(solution)/shard_map/gather | solution.py:40
  30.8 7.2 %reshape.83 = bf16[32,1,36,2048]{3,2,0,1:T(8,128)(2,1)} reshape(bf16[1152,2048]{1,0:T(8,128)(2,1)} %gather_fusion) | data formatting | bytes 9437184 | tf_op jit(solution)/shard_map/reshape | solution.py:40
  38.0 0.0 copy-start
  38.0 8.1 %all-to-all-start = ((bf16[32,1,36,2048]{3,2,1,0:T(8,128)(2,1)}), bf16[32,1,36,2048]{3,2,1,0:T(8,128)(2,1)}, u32[]{:S(2)}, u32[]{:S(2)}) async-start(bf16[32,1,36,2048]{3,2,1,0:T(8,128)(2,1)} %bitcast.75), calls=%async_computation | async-start | bytes 10485760 | tf_op jit(solution)/shard_map/all_to_all | solution.py:41
  46.1 0.0 all-gather.5.cloned.1.call-start
  46.1 0.0 copy-done
  46.1 0.9 convert_element_type.35
  47.0 0.0 all-gather.5.cloned.1.call-update
  47.0 62.8 %all-to-all-done = bf16[32,1,36,2048]{3,2,1,0:T(8,128)(2,1)} async-done(((bf16[32,1,36,2048]{3,2,1,0:T(8,128)(2,1)}), bf16[32,1,36,2048]{3,2,1,0:T(8,128)(2,1)}, u32[]{:S(2)}, u32[]{:S(2)}) %all-to-all-start) | async-done | bytes 4718624 | tf_op jit(solution)/shard_map/all_to_all | solution.py:41
  109.9 0.0 all-gather.3.cloned.1.call-done
  109.9 17.5 %fusion.4 = f32[32,1,36,2048]{3,2,0,1:T(8,128)} fusion(bf16[1,2048,2048]{2,1,0:T(8,128)(2,1)} %all-gather.3.cloned.1.call-done, bf16[32,1,36,2048]{3,2,1,0:T(8,128)(2,1)} %all-to-all-done), kind=kOutput, calls=%fused_computation.9 | convolution fusion | flops 9663676416 | bytes 22544384 | tf_op jit(solution)/shard_map/secd,edf->secf/dot_general | solution.py:42
  127.4 34.5 %all-gather.5.cloned.1.call-done = bf16[1,1024,2048]{2,1,0:T(8,128)(2,1)} async-done(((bf16[1,128,2048]{2,1,0:T(8,128)(2,1)}), bf16[1,1024,2048]{2,1,0:T(8,128)(2,1)}) %all-gather.5.cloned.1.call-update) | async-done | bytes 4194320 | tf_op jit(solution)/shard_map/all_gather | solution.py:22
  161.8 11.3 %convert_bitcast_fusion = bf16[32,1,36,2048]{3,2,1,0:T(8,128)(2,1)} fusion(bf16[1,1024,2048]{2,1,0:T(8,128)(2,1)} %all-gather.5.cloned.1.call-done, f32[32,1,36,2048]{3,2,0,1:T(8,128)} %fusion.4), kind=kOutput, calls=%fused_computation.8 | convolution fusion | flops 4841275392 | bytes 18350080 | tf_op jit(solution)/shard_map/secf,efd->secd/dot_general | solution.py:46
  173.1 0.0 copy-start.2
  173.1 7.9 %all-to-all-start.1 = ((bf16[32,1,36,2048]{3,2,1,0:T(8,128)(2,1)}), bf16[32,1,36,2048]{3,2,1,0:T(8,128)(2,1)}, u32[]{:S(2)}, u32[]{:S(2)}) async-start(bf16[32,1,36,2048]{3,2,1,0:T(8,128)(2,1)} %convert_bitcast_fusion), calls=%async_computation.1 | async-start | bytes 10485760 | tf_op jit(solution)/shard_map/all_to_all | solution.py:50
  181.0 0.0 copy-done.2
  181.0 0.1 copy.21
  181.2 63.6 %all-to-all-done.1 = bf16[32,1,36,2048]{3,2,1,0:T(8,128)(2,1)} async-done(((bf16[32,1,36,2048]{3,2,1,0:T(8,128)(2,1)}), bf16[32,1,36,2048]{3,2,1,0:T(8,128)(2,1)}, u32[]{:S(2)}, u32[]{:S(2)}) %all-to-all-start.1) | async-done | bytes 4718624 | tf_op jit(solution)/shard_map/all_to_all | solution.py:50
  244.8 7.2 %copy.29 = bf16[32,1,36,2048]{3,0,2,1:T(8,128)(2,1)} copy(bf16[32,1,36,2048]{3,2,1,0:T(8,128)(2,1)} %all-to-all-done.1) | data formatting | bytes 9437184 | tf_op jit(solution)/shard_map/all_to_all | solution.py:50
  252.1 25.4 %gather_fusion.1 = bf16[1024,2048]{1,0:T(8,128)(2,1)} fusion(bf16[32,36,2048]{2,0,1:T(8,128)(2,1)} %bitcast.73, s32[1024]{0:T(1024)S(1)} %bitcast.74), kind=kCustom, calls=%fused_computation.1 | custom fusion | bytes 8396800 | tf_op jit(solution)/shard_map/gather | solution.py:52
  277.4 3.4 %fusion.9 = bf16[128,1,2048]{2,1,0:T(2,128)(2,1)S(1)} fusion(bf16[128,8,1]{1,2,0:T(2,128)(2,1)S(1)} %copy.21, bf16[1024,2048]{1,0:T(8,128)(2,1)} %gather_fusion.1), kind=kOutput, calls=%fused_computation.11 | convolution fusion | flops 4194304 | bytes 4720640 | tf_op jit(solution)/shard_map/tk,tkd->td/dot_general | solution.py:53
  280.8 1.1 copy.30
  (9 shorter events, 0.2 us)
Async XLA Ops:
  6.5 13.5 %copy-start.4 = (s32[2]{0:T(128)S(1)}, s32[2]{0:T(128)}, u32[]{:S(2)}) copy-start(s32[2]{0:T(128)} %constant.45) | copy-start | bytes 28
  6.5 13.5 %copy-start.3 = (s32[2]{0:T(128)S(1)}, s32[2]{0:T(128)}, u32[]{:S(2)}) copy-start(s32[2]{0:T(128)} %constant.48) | copy-start | bytes 28
  6.5 18.2 %copy-start.1 = (bf16[1,128,2048]{2,1,0:T(8,128)(2,1)S(1)}, bf16[1,128,2048]{2,1,0:T(8,128)(2,1)}, u32[]{:S(2)}) copy-start(bf16[1,128,2048]{2,1,0:T(8,128)(2,1)} %param.5) | copy-start | bytes 1572868
  6.5 103.3 %all-gather.3.cloned.1.call-start = ((), (), s32[]{:S(2)}) async-start(), calls=%async_computation.2 | async-start | bytes 9437184 | tf_op jit(solution)/shard_map/all_gather | solution.py:21
  38.0 8.1 %copy-start = (f32[1,128,2048]{2,1,0:T(8,128)S(1)}, f32[1,128,2048]{2,1,0:T(8,128)}, u32[]{:S(2)}) copy-start(f32[1,128,2048]{2,1,0:T(8,128)} %param.9) | copy-start | bytes 3145732
  38.0 71.9 %all-to-all-start = ((bf16[32,1,36,2048]{3,2,1,0:T(8,128)(2,1)}), bf16[32,1,36,2048]{3,2,1,0:T(8,128)(2,1)}, u32[]{:S(2)}, u32[]{:S(2)}) async-start(bf16[32,1,36,2048]{3,2,1,0:T(8,128)(2,1)} %bitcast.75), calls=%async_computation | async-start | bytes 10485760 | tf_op jit(solution)/shard_map/all_to_all | solution.py:41
  46.1 115.7 %all-gather.5.cloned.1.call-start = ((), (), s32[]{:S(2)}) async-start(), calls=%async_computation.3 | async-start | bytes 4718592 | tf_op jit(solution)/shard_map/all_gather | solution.py:22
  173.1 7.9 %copy-start.2 = (f32[1,128,8]{1,2,0:T(8,128)S(1)}, f32[1,128,8]{1,2,0:T(8,128)}, u32[]{:S(2)}) copy-start(f32[1,128,8]{1,2,0:T(8,128)} %param.7) | copy-start | bytes 12292
  173.1 71.7 %all-to-all-start.1 = ((bf16[32,1,36,2048]{3,2,1,0:T(8,128)(2,1)}), bf16[32,1,36,2048]{3,2,1,0:T(8,128)(2,1)}, u32[]{:S(2)}, u32[]{:S(2)}) async-start(bf16[32,1,36,2048]{3,2,1,0:T(8,128)(2,1)} %convert_bitcast_fusion), calls=%async_computation.1 | async-start | bytes 10485760 | tf_op jit(solution)/shard_map/all_to_all | solution.py:50
Sparse Core Ops, SparseCore 0:
  9.5 96.9 all-gather.2
  108.3 53.4 all-gather.4
where the time goes:
time: 290 us; the launch traced here: 289 us
  waiting for transfers between devices  161 us (56%)
  local copies, waits for them, and re-layouts  53 us (18%)
  matrix products  32.2 us (11%)
  starting transfers between devices  16 us (6%)
  between operations  13.6 us (5%)
  other arithmetic  13.1 us (5%)
    all_to_all x1, waiting for transfers between devices, per_device(): lax.all_to_all(expert_out, 'tok', split_axis=0, concat_axis=0, tiled=True)  63.6 us
    all_to_all x1, waiting for transfers between devices, per_device(): lax.all_to_all(send_rows, 'tok', split_axis=0, concat_axis=0, tiled=True)  62.8 us
    all_gather x1, waiting for transfers between devices, per_device(): lax.all_gather(served_down, 'rep', axis=1, tiled=True)  34.5 us
    gather x1, local copies, waits for them, and re-layouts, per_device(): returned[flat_picks, slot_index]  25.4 us
    dot_general x1, matrix products, per_device(): jnp.einsum('secd,edf->secf', arrived, full_gate, preferred_element_type=j...  17.5 us
    dot_general x1, matrix products, per_device(): jnp.einsum('secf,efd->secd', hidden_units, full_down, preferred_element_t...  11.3 us
    another operation x3, other arithmetic  9.15 us
    all_to_all x1, starting transfers between devices, per_device(): lax.all_to_all(send_rows, 'tok', split_axis=0, concat_axis=0, tiled=True)  8.06 us
  transfers between devices with their start and end apart: 4, of which 3 were waited for; matrix products, arithmetic and copies ran while one was open for 16% of the time, Pallas kernels for 0%

commit v1 on v0

--- a/solution.py
+++ b/solution.py
@@ -4,6 +4,11 @@
 from jax.sharding import PartitionSpec as P
 
 CAP = 36
+
+
+def exchange_gather(x, mesh_axis, dim):
+    sent = jnp.stack([x] * lax.axis_size(mesh_axis))
+    return jnp.concatenate(lax.all_to_all(sent, mesh_axis, 0, 0), axis=dim)
 
 
 def per_device(hidden_states, routes, gate_prob, gate_up, down):
@@ -19,7 +24,7 @@
     unit_count = served_gate.shape[2] // 2
     full_gate, full_down = (
         lax.all_gather(served_gate, "rep", axis=1, tiled=True),
-        lax.all_gather(served_down, "rep", axis=1, tiled=True),
+        exchange_gather(served_down, "rep", 1),
     )
     flat_picks = routes[0].reshape(-1)
     pick_count = flat_picks.shape[0]

time: 290 us -> 343 us (1.18)
  waiting for transfers between devices: 161 us -> 205 us
  starting transfers between devices: 16 us -> 22.7 us
    all_to_all x0 -> x1, waiting for transfers between devices: none -> 78.1 us  [exchange_gather(): return jnp.concatenate(lax.all_to_all(sent, mesh_axis, 0, 0), axis=dim)]
    all_gather x1 -> x0, waiting for transfers between devices: 34.5 us -> none  [per_device(): lax.all_gather(served_down, 'rep', axis=1, tiled=True)]
    all_to_all x0 -> x1, starting transfers between devices: none -> 8.19 us  [exchange_gather(): return jnp.concatenate(lax.all_to_all(sent, mesh_axis, 0, 0), axis=dim)]
  transfers between devices with their start and end apart: 4 -> 4, of which waited for: 3 -> 3; matrix products, arithmetic and copies ran while one was open for 16% -> 14% of each run, Pallas kernels for 0% -> 0%
where the time goes in v1:
time: 343 us; the launch traced here: 342 us
  waiting for transfers between devices  205 us (60%)
  local copies, waits for them, and re-layouts  55.6 us (16%)
  matrix products  32.1 us (9%)
  starting transfers between devices  22.7 us (7%)
  between operations  13.6 us (4%)
  other arithmetic  12.3 us (4%)
    all_to_all x1, waiting for transfers between devices, exchange_gather(): return jnp.concatenate(lax.all_to_all(sent, mesh_axis, 0, 0), axis=dim)  78.1 us
    all_to_all x1, waiting for transfers between devices, per_device(): lax.all_to_all(send_rows, 'tok', split_axis=0, concat_axis=0, tiled=True)  63.7 us
    all_to_all x1, waiting for transfers between devices, per_device(): lax.all_to_all(expert_out, 'tok', split_axis=0, concat_axis=0, tiled=True)  63.6 us
    gather x1, local copies, waits for them, and re-layouts, per_device(): returned[flat_picks, slot_index]  25.4 us
    dot_general x1, matrix products, per_device(): jnp.einsum('secd,edf->secf', arrived, full_gate, preferred_element_type=j...  17.4 us
    dot_general x1, matrix products, per_device(): jnp.einsum('secf,efd->secd', hidden_units, full_down, preferred_element_t...  11.3 us
    another operation x3, other arithmetic  9.15 us
    all_to_all x1, starting transfers between devices, exchange_gather(): return jnp.concatenate(lax.all_to_all(sent, mesh_axis, 0, 0), axis=dim)  8.19 us
  transfers between devices with their start and end apart: 4, of which 3 were waited for; matrix products, arithmetic and copies ran while one was open for 14% of the time, Pallas kernels for 0%

profile of v1, /device:TPU:7, one launch (start us, length us, event | category | flops | bytes accessed | tf_op | source)
XLA Modules:
  0.0 341.7 jit_solution(3079459023881840418)
XLA Ops:
  6.5 0.0 copy-start.4
  6.5 0.0 copy-start.3
  6.5 0.0 copy-start.1
  6.5 0.0 all-gather.2.cloned.1.call-start
  6.5 2.8 convert_element_type.35
  9.3 0.0 all-gather.2.cloned.1.call-update
  9.4 0.8 copy.13
  10.2 0.1 eq.29
  10.3 0.1 eq.25
  10.3 0.1 reshape_squeeze.3
  10.5 9.0 %reduce-window.6 = s32[32,8,128]{2,1,0:T(8,128)S(1)} reduce-window(s32[32,8,128]{2,1,0:T(8,128)S(1)} %fusion.17, s32[]{:T(128)} %constant.29.clone.1), window={size=1x1x128 pad=0_0x0_0x127_0}, to_apply=%region_0.0 | reduce-window | flops 4161536 | bytes 262148 | tf_op jit(solution)/shard_map/reduce-window
  19.5 0.1 slice.20
  19.6 0.1 copy.16
  19.7 0.1 copy.17
  19.8 0.1 broadcast_add_fusion
  20.0 0.0 copy-done.4
  20.0 0.1 multiply_reduce_fusion
  20.1 0.0 copy-done.3
  20.1 0.1 and_reduce_fusion
  20.2 4.3 %scatter_custom_fusion = s32[1152]{0:T(1024)S(1)} fusion(s32[1024]{0:T(1024)S(1)} %get-tuple-element.9, s32[1024]{0:T(1024)S(1)} %get-tuple-element.8, s32[]{:T(128)} %constant.28.clone.1), kind=kCustom, calls=%fused_computation.39 | custom fusion | bytes 4612
  24.5 0.1 reshape.98
  24.7 0.1 reshape.101
  24.8 0.0 copy-done.1
  24.8 6.0 %gather_fusion = bf16[1152,2048]{1,0:T(8,128)(2,1)} fusion(bf16[129,2048]{1,0:T(8,128)(2,1)S(1)} %concatenate.7, s32[2048]{0:T(1024)S(1)} %pad_clamp_fusion), kind=kCustom, calls=%fused_computation | custom fusion | bytes 9441792 | tf_op jit(solution)/shard_map/gather | solution.py:45
  30.8 7.2 %reshape.88 = bf16[32,1,36,2048]{3,2,0,1:T(8,128)(2,1)} reshape(bf16[1152,2048]{1,0:T(8,128)(2,1)} %gather_fusion) | data formatting | bytes 9437184 | tf_op jit(solution)/shard_map/reshape | solution.py:45
  38.0 0.0 copy-start
  38.0 8.1 %all-to-all-start = ((bf16[32,1,36,2048]{3,2,1,0:T(8,128)(2,1)}), bf16[32,1,36,2048]{3,2,1,0:T(8,128)(2,1)}, u32[]{:S(2)}, u32[]{:S(2)}) async-start(bf16[32,1,36,2048]{3,2,1,0:T(8,128)(2,1)} %bitcast.75), calls=%async_computation | async-start | bytes 10485760 | tf_op jit(solution)/shard_map/all_to_all | solution.py:46
  46.1 0.0 copy-done
  46.1 0.1 convert_bitcast_fusion.1
  46.2 63.7 %all-to-all-done = bf16[32,1,36,2048]{3,2,1,0:T(8,128)(2,1)} async-done(((bf16[32,1,36,2048]{3,2,1,0:T(8,128)(2,1)}), bf16[32,1,36,2048]{3,2,1,0:T(8,128)(2,1)}, u32[]{:S(2)}, u32[]{:S(2)}) %all-to-all-start) | async-done | bytes 4718624 | tf_op jit(solution)/shard_map/all_to_all | solution.py:46
  109.9 2.6 stack.2
  112.5 8.2 %all-to-all-start.1 = ((bf16[8,1,128,2048]{3,2,1,0:T(8,128)(2,1)}), bf16[8,1,128,2048]{3,2,1,0:T(8,128)(2,1)}, u32[]{:S(2)}, u32[]{:S(2)}) async-start(bf16[8,1,128,2048]{3,2,1,0:T(8,128)(2,1)} %stack.2), calls=%async_computation.1 | async-start | bytes 8388608 | tf_op jit(solution)/shard_map/all_to_all | solution.py:11
  120.7 0.0 all-gather.2.cloned.1.call-done
  120.7 17.4 %fusion.4 = f32[32,1,36,2048]{3,2,0,1:T(8,128)} fusion(bf16[1,2048,2048]{2,1,0:T(8,128)(2,1)} %all-gather.2.cloned.1.call-done, bf16[32,1,36,2048]{3,2,1,0:T(8,128)(2,1)} %all-to-all-done), kind=kOutput, calls=%fused_computation.9 | convolution fusion | flops 9663676416 | bytes 22544384 | tf_op jit(solution)/shard_map/secd,edf->secf/dot_general | solution.py:47
  138.1 78.1 %all-to-all-done.1 = bf16[8,1,128,2048]{3,2,1,0:T(8,128)(2,1)} async-done(((bf16[8,1,128,2048]{3,2,1,0:T(8,128)(2,1)}), bf16[8,1,128,2048]{3,2,1,0:T(8,128)(2,1)}, u32[]{:S(2)}, u32[]{:S(2)}) %all-to-all-start.1) | async-done | bytes 4194336 | tf_op jit(solution)/shard_map/all_to_all | solution.py:11
  216.2 11.3 %convert_bitcast_fusion = bf16[32,1,36,2048]{3,2,1,0:T(8,128)(2,1)} fusion(bf16[1024,2048,1]{1,0,2:T(8,128)(2,1)} %bitcast.16, f32[32,1,36,2048]{3,2,0,1:T(8,128)} %fusion.4), kind=kOutput, calls=%fused_computation.8 | convolution fusion | flops 4841275392 | bytes 18350080 | tf_op jit(solution)/shard_map/secf,efd->secd/dot_general | solution.py:51
  227.5 0.0 copy-start.2
  227.5 6.4 %all-to-all-start.2 = ((bf16[32,1,36,2048]{3,2,1,0:T(8,128)(2,1)}), bf16[32,1,36,2048]{3,2,1,0:T(8,128)(2,1)}, u32[]{:S(2)}, u32[]{:S(2)}) async-start(bf16[32,1,36,2048]{3,2,1,0:T(8,128)(2,1)} %convert_bitcast_fusion), calls=%async_computation.2 | async-start | bytes 10485760 | tf_op jit(solution)/shard_map/all_to_all | solution.py:55
  233.9 0.0 copy-done.2
  234.0 0.1 copy.21
  234.1 63.6 %all-to-all-done.2 = bf16[32,1,36,2048]{3,2,1,0:T(8,128)(2,1)} async-done(((bf16[32,1,36,2048]{3,2,1,0:T(8,128)(2,1)}), bf16[32,1,36,2048]{3,2,1,0:T(8,128)(2,1)}, u32[]{:S(2)}, u32[]{:S(2)}) %all-to-all-start.2) | async-done | bytes 4718624 | tf_op jit(solution)/shard_map/all_to_all | solution.py:55
  297.7 7.2 %copy.29 = bf16[32,1,36,2048]{3,0,2,1:T(8,128)(2,1)} copy(bf16[32,1,36,2048]{3,2,1,0:T(8,128)(2,1)} %all-to-all-done.2) | data formatting | bytes 9437184 | tf_op jit(solution)/shard_map/all_to_all | solution.py:55
  305.0 25.4 %gather_fusion.1 = bf16[1024,2048]{1,0:T(8,128)(2,1)} fusion(bf16[32,36,2048]{2,0,1:T(8,128)(2,1)} %bitcast.73, s32[1024]{0:T(1024)S(1)} %bitcast.74), kind=kCustom, calls=%fused_computation.1 | custom fusion | bytes 8396800 | tf_op jit(solution)/shard_map/gather | solution.py:57
  330.4 3.4 fusion.9
  333.8 1.1 copy.30
  (9 shorter events, 0.2 us)
Async XLA Ops:
  6.5 13.5 %copy-start.4 = (s32[2]{0:T(128)S(1)}, s32[2]{0:T(128)}, u32[]{:S(2)}) copy-start(s32[2]{0:T(128)} %constant.45) | copy-start | bytes 28
  6.5 13.6 %copy-start.3 = (s32[2]{0:T(128)S(1)}, s32[2]{0:T(128)}, u32[]{:S(2)}) copy-start(s32[2]{0:T(128)} %constant.48) | copy-start | bytes 28
  6.5 18.2 %copy-start.1 = (bf16[1,128,2048]{2,1,0:T(8,128)(2,1)S(1)}, bf16[1,128,2048]{2,1,0:T(8,128)(2,1)}, u32[]{:S(2)}) copy-start(bf16[1,128,2048]{2,1,0:T(8,128)(2,1)} %param.5) | copy-start | bytes 1572868
  6.5 114.1 %all-gather.2.cloned.1.call-start = ((), (), s32[]{:S(2)}) async-start(), calls=%async_computation.3 | async-start | bytes 9437184 | tf_op jit(solution)/shard_map/all_gather | solution.py:26
  38.0 8.1 %copy-start = (f32[1,128,2048]{2,1,0:T(8,128)S(1)}, f32[1,128,2048]{2,1,0:T(8,128)}, u32[]{:S(2)}) copy-start(f32[1,128,2048]{2,1,0:T(8,128)} %param.9) | copy-start | bytes 3145732
  38.0 71.9 %all-to-all-start = ((bf16[32,1,36,2048]{3,2,1,0:T(8,128)(2,1)}), bf16[32,1,36,2048]{3,2,1,0:T(8,128)(2,1)}, u32[]{:S(2)}, u32[]{:S(2)}) async-start(bf16[32,1,36,2048]{3,2,1,0:T(8,128)(2,1)} %bitcast.75), calls=%async_computation | async-start | bytes 10485760 | tf_op jit(solution)/shard_map/all_to_all | solution.py:46
  112.5 103.7 %all-to-all-start.1 = ((bf16[8,1,128,2048]{3,2,1,0:T(8,128)(2,1)}), bf16[8,1,128,2048]{3,2,1,0:T(8,128)(2,1)}, u32[]{:S(2)}, u32[]{:S(2)}) async-start(bf16[8,1,128,2048]{3,2,1,0:T(8,128)(2,1)} %stack.2), calls=%async_computation.1 | async-start | bytes 8388608 | tf_op jit(solution)/shard_map/all_to_all | solution.py:11
  227.5 6.5 %copy-start.2 = (f32[1,128,8]{1,2,0:T(8,128)S(1)}, f32[1,128,8]{1,2,0:T(8,128)}, u32[]{:S(2)}) copy-start(f32[1,128,8]{1,2,0:T(8,128)} %param.7) | copy-start | bytes 12292
  227.5 70.2 %all-to-all-start.2 = ((bf16[32,1,36,2048]{3,2,1,0:T(8,128)(2,1)}), bf16[32,1,36,2048]{3,2,1,0:T(8,128)(2,1)}, u32[]{:S(2)}, u32[]{:S(2)}) async-start(bf16[32,1,36,2048]{3,2,1,0:T(8,128)(2,1)} %convert_bitcast_fusion), calls=%async_computation.2 | async-start | bytes 10485760 | tf_op jit(solution)/shard_map/all_to_all | solution.py:55
Sparse Core Ops, SparseCore 0:
  9.5 96.9 all-gather.1
